TPU v7x, 32 devices: a whole 2x2x4 slice. The times are simulated.
32 devices in a mesh: wide: 8 (over z, core), narrow: 4 (over y, x).
Axes of the slice: x: 2, y: 2, z: 4, core: 2. Of those that a mesh axis runs over, the one named last changes fastest.
Arguments:
- traction: float32 [3, 64, 49152], P(None, None, ('wide', 'narrow')), may hold values from -6 to 6
- near_kernel: bfloat16 [96, 4, 512, 512], P(('wide', 'narrow')), may hold values from -0.125 to 0.125
- neighbours: int32 [96, 4], P(('wide', 'narrow')), may hold values from 0 to 95, as said below
- far_basis: bfloat16 [5, 49152, 128], P(None, ('wide', 'narrow')), may hold values from -4 to 4
- surface_gap: float32 [3, 49152], P(None, ('wide', 'narrow')), may hold values from -3 to 3
- friction: float32 [49152], P(('wide', 'narrow')), may hold values from 0.2 to 1
- contact_flags: int32 [49152], P(('wide', 'narrow')), may hold values 0 or 1
- cluster_order: int32 [49152], P(('wide', 'narrow')), may hold values from 0 to 49151, as said below
- approach: float32 [3, 64], replicated, may hold values from -1 to 2
Outputs:
- traction_new: float32 [3, 64, 49152], P(None, None, ('wide', 'narrow'))
- residual: float32 [3, 64, 49152], P(None, None, ('wide', 'narrow'))
- step_size: float32 [64], replicated
Inputs may be any that keep to these rules, and one draw needn't show every extreme that they name: `neighbours`: entry 0 of row b is b itself; the other 3 entries are distinct blocks other than b, each within 3 blocks of b. `cluster_order`: a permutation of the panels that maps every aligned group of 1536 panels onto itself.
All inputs are finite; a program needn't handle non-finite values. No bound on the sum of `contact_flags` on one device may be relied on, other than what follows from the above.
Results may differ from a plain program's by a relative error of at most 0.0034.
Values may be sent and summed in bfloat16 or wider, within the bound.
A program may use at most 64 MiB of HBM per device.

v0:
```python
import math

import jax
import jax.numpy as jnp
from jax import lax
from jax.sharding import PartitionSpec as P

SLIP_EPS = 0.01


def extended(cells, sides, width):
    for axis, dim in sides:
        count = lax.axis_size(axis)
        ends = count - 1
        head = lax.slice_in_dim(cells, 0, width, axis=dim)
        tail = lax.slice_in_dim(cells, cells.shape[dim] - width, cells.shape[dim], axis=dim)
        cells = jnp.concatenate(
            [
                lax.ppermute(tail, axis, [(i, (i + 1) % count) for i in range(ends)]),
                cells,
                lax.ppermute(head, axis, [((i + 1) % count, i) for i in range(ends)]),
            ],
            axis=dim,
        )
    return cells


def from_partner(block, axis, stride):
    count = lax.axis_size(axis)
    route = []
    for low in range(count):
        high = low | 1 << stride
        if high != low and high < count:
            route += [(low, high), (high, low)]
    return lax.ppermute(block, axis, route)


def near_field(field_low, near_kernel, neighbours):
    row_count, panel_count = field_low.shape
    blk_dev = near_kernel.shape[0]
    block_len = near_kernel.shape[2]
    padded = extended(field_low, ((("wide", "narrow"), 1),), panel_count)
    blocks = padded.reshape(row_count, 3 * blk_dev, block_len)
    local_ids = jnp.arange(blk_dev, dtype=jnp.int32)
    ext_slots = neighbours - neighbours[:, :1] + local_ids[:, None] + blk_dev
    picked = jnp.take(blocks, ext_slots.reshape(-1), axis=1)
    picked = picked.reshape(row_count, blk_dev, neighbours.shape[1], block_len)
    result = jnp.einsum("bkij,xbkj->xbi", near_kernel, picked, preferred_element_type=jnp.float32)
    return result.reshape(row_count, panel_count)


def tree_totals(coeffs):
    narrow_bits = lax.axis_size("narrow").bit_length() - 1
    wide_bits = lax.axis_size("wide").bit_length() - 1
    for bit_pos in range(narrow_bits + wide_bits):
        partner = from_partner(coeffs[bit_pos:], ("wide", "narrow"), bit_pos)
        coeffs = jnp.concatenate([coeffs[:bit_pos], coeffs[bit_pos:] + partner], axis=0)
    return coeffs


def level_gains(panel_count, level_count, rank_len):
    gain_list = [
        0.64 / math.sqrt(rank_len * panel_count * 2 ** (tree_level + 1))
        for tree_level in range(level_count)
    ]
    return jnp.array(gain_list, jnp.float32)


def far_field(field_low, far_basis):
    coeffs = jnp.einsum("xp,lpr->lxr", field_low, far_basis, preferred_element_type=jnp.float32)
    summed = tree_totals(coeffs)
    gains = level_gains(field_low.shape[1], far_basis.shape[0], far_basis.shape[2])
    scaled = (summed * gains[:, None, None]).astype(jnp.bfloat16)
    return jnp.einsum("lxr,lpr->xp", scaled, far_basis, preferred_element_type=jnp.float32)


def apply_operator(field, near_kernel, neighbours, far_basis):
    field_low = field.astype(jnp.bfloat16)
    return near_field(field_low, near_kernel, neighbours) + far_field(field_low, far_basis)


def project_cone(trial_point, mu_sorted):
    normal = trial_point[0]
    slide_a = trial_point[1]
    slide_b = trial_point[2]
    slip = jnp.sqrt(slide_a * slide_a + slide_b * slide_b + SLIP_EPS)
    coeff = mu_sorted[None, :]
    stick = slip <= coeff * normal
    pressed = jnp.where(
        stick, normal, jnp.maximum((normal + coeff * slip) / (1.0 + coeff * coeff), 0.0)
    )
    factor = jnp.where(stick, jnp.ones_like(slip), coeff * pressed / slip)
    return jnp.stack([pressed, factor * slide_a, factor * slide_b])


def body(
    traction,
    near_kernel,
    neighbours,
    far_basis,
    surface_gap,
    friction,
    contact_flags,
    cluster_order,
    approach,
):
    comp_count, load_count, panel_count = traction.shape
    row_count = comp_count * load_count
    local_order = cluster_order % panel_count
    gap_sorted = jnp.take(surface_gap, local_order, axis=1)
    mu_sorted = jnp.take(friction, local_order)
    live_mask = jnp.take(contact_flags, local_order).astype(jnp.float32)
    target = (approach[:, :, None] - gap_sorted[:, None, :]).reshape(row_count, panel_count)
    state_rows = traction.reshape(row_count, panel_count)
    residual = apply_operator(state_rows, near_kernel, neighbours, far_basis) - target
    image_rows = apply_operator(residual, near_kernel, neighbours, far_basis)
    residual_out = residual.reshape(comp_count, load_count, panel_count)
    image_out = image_rows.reshape(comp_count, load_count, panel_count)
    cross_local = jnp.sum(residual_out * image_out, axis=(0, 2))
    square_local = jnp.sum(image_out * image_out, axis=(0, 2))
    cross_sum, square_sum = lax.psum((cross_local, square_local), ("wide", "narrow"))
    entries = comp_count * panel_count * lax.axis_size(("wide", "narrow"))
    step_size = cross_sum / entries / (square_sum / entries + 1e-06)
    trial_point = traction - step_size[None, :, None] * residual_out
    updated = project_cone(trial_point, mu_sorted) * live_mask[None, None, :]
    return (updated, residual_out, step_size)


def solution(mesh):
    return jax.shard_map(
        body,
        mesh=mesh,
        in_specs=(
            P(None, None, ("wide", "narrow")),
            P(("wide", "narrow"), None, None, None),
            P(("wide", "narrow"), None),
            P(None, ("wide", "narrow"), None),
            P(None, ("wide", "narrow")),
            P(("wide", "narrow")),
            P(("wide", "narrow")),
            P(("wide", "narrow")),
            P(),
        ),
        out_specs=(P(None, None, ("wide", "narrow")), P(None, None, ("wide", "narrow")), P()),
        check_vma=False,
    )
```

profile of v0, /device:TPU:0, one launch (start us, length us, event | category | flops | bytes accessed | tf_op | source)
XLA Modules:
  0.0 200.1 jit_solution(18257478556729925627)
XLA Ops:
  0.6 1.5 convert_element_type.20
  3.4 6.3 %collective-permute-start = (bf16[192,1536]{1,0:T(8,128)(2,1)S(1)}, bf16[192,1536]{1,0:T(8,128)(2,1)}, u32[]{:S(2)}, u32[]{:S(2)}) collective-permute-start(bf16[192,1536]{1,0:T(8,128)(2,1)S(1)} %bitcast.63), channel_id=1, source_target_pairs={{0,1},{1,2},{2,3},{3,4},{4,5},{5,6},{6,7},{7,8},{8,9},{9,10},{10,1... | collective-permute-start | bytes 1769480 | tf_op jit(solution)/shard_map/ppermute | solution.py:19
  9.8 1.4 convolution_bitcast_fusion.4
  11.2 2.1 %collective-permute-start.2 = (f32[5,192,128]{2,1,0:T(8,128)}, f32[5,192,128]{2,1,0:T(8,128)}, u32[]{:S(2)}, u32[]{:S(2)}) collective-permute-start(f32[5,192,128]{2,1,0:T(8,128)} %convolution_bitcast_fusion.4), channel_id=1, source_target_pairs={{0,1},{1,0},{2,3},{3,2},{4,5},{5,4},{6,7},{7,6},{8,9},{9,8},{10,11... | collective-permute-start | bytes 1474568 | tf_op jit(solution)/shard_map/ppermute | solution.py:35
  13.7 3.7 %gather_fusion = f32[1536,3]{1,0:T(8,128)} fusion(f32[3,1536]{0,1:T(8,128)S(1)} %copy.40, s32[2048]{0:T(1024)S(1)} %pad_clamp_fusion), kind=kCustom, calls=%fused_computation.2 | custom fusion | bytes 43008 | tf_op jit(solution)/shard_map/jit(_take)/gather | solution.py:110
  17.4 8.4 %gather_fusion.2 = s32[1536]{0:T(1024)S(1)} fusion(s32[1536]{0:T(1024)S(1)} %copy-done.1, s32[2048]{0:T(1024)S(1)} %pad_clamp_fusion), kind=kCustom, calls=%fused_computation.4 | custom fusion | bytes 18432 | tf_op jit(solution)/shard_map/jit(_take)/gather | solution.py:112
  29.0 14.6 %collective-permute-done.2 = f32[5,192,128]{2,1,0:T(8,128)} collective-permute-done((f32[5,192,128]{2,1,0:T(8,128)}, f32[5,192,128]{2,1,0:T(8,128)}, u32[]{:S(2)}, u32[]{:S(2)}) %collective-permute-start.2) | collective-permute-done | bytes 491552 | tf_op jit(solution)/shard_map/ppermute | solution.py:35
  45.7 2.6 %pad_maximum_fusion = bf16[192,4608]{1,0:T(8,128)(2,1)} fusion(bf16[192,1536]{1,0:T(8,128)(2,1)} %collective-permute-done.1, bf16[192,1536]{1,0:T(8,128)(2,1)S(1)} %bitcast.65, bf16[192,1536]{1,0:T(8,128)(2,1)} %collective-permute-done), kind=kLoop, calls=%fused_computation.12 | loop fusion | flops 5308416 | bytes 3538944 | tf_op jit(solution)/shard_map/concatenate | solution.py:17
  48.2 4.0 %copy.37 = bf16[192,4608]{0,1:T(8,128)(2,1)} copy(bf16[192,4608]{1,0:T(8,128)(2,1)} %pad_maximum_fusion) | data formatting | bytes 3538944 | tf_op jit(solution)/shard_map/concatenate | solution.py:17
  52.2 4.0 %copy.38 = bf16[192,9,512]{2,0,1:T(8,128)(2,1)} copy(bf16[192,9,512]{0,2,1:T(8,128)(2,1)} %bitcast.60) | data formatting | bytes 3538944 | tf_op jit(solution)/shard_map/reshape | solution.py:43
  56.3 3.7 %gather_fusion.3 = bf16[12,192,512]{2,1,0:T(8,128)(2,1)} fusion(bf16[192,9,512]{2,0,1:T(8,128)(2,1)} %copy.38, s32[1024]{0:T(1024)S(1)} %pad_clamp_fusion.1), kind=kCustom, calls=%fused_computation.clone | custom fusion | bytes 4718640 | tf_op jit(solution)/shard_map/jit(_take)/gather | solution.py:46
  61.4 2.0 broadcast_select_fusion.1
  63.4 2.5 %collective-permute-start.5 = (f32[2,192,128]{2,1,0:T(8,128)S(1)}, f32[2,192,128]{2,1,0:T(8,128)S(1)}, u32[]{:S(2)}, u32[]{:S(2)}) collective-permute-start(f32[2,192,128]{2,1,0:T(8,128)S(1)} %slice.102), channel_id=1, source_target_pairs={{0,8},{8,0},{1,9},{9,1},{2,10},{10,2},{3,11},{11,3},{4,12},{12,4},... | collective-permute-start | bytes 589832 | tf_op jit(solution)/shard_map/ppermute | solution.py:35
  65.9 5.0 %convolution_bitcast_fusion.3 = f32[3,24,8,512]{3,2,1,0:T(8,128)S(1)} fusion(bf16[192,3,4,512]{3,0,2,1:T(8,128)(2,1)S(1)} %bitcast.59, bf16[3,4,512,512]{3,2,1,0:T(8,128)(2,1)} %param.14), kind=kOutput, calls=%fused_computation.15 | convolution fusion | flops 1207959552 | bytes 9830400 | tf_op jit(solution)/shard_map/bkij,xbkj->xbi/dot_general | solution.py:48
  71.5 2.8 %collective-permute-start.6 = (f32[1,192,128]{2,1,0:T(8,128)S(1)}, f32[1,192,128]{2,1,0:T(8,128)S(1)}, u32[]{:S(2)}, u32[]{:S(2)}) collective-permute-start(f32[1,192,128]{2,1,0:T(8,128)S(1)} %slice.103), channel_id=1, source_target_pairs={{0,16},{16,0},{1,17},{17,1},{2,18},{18,2},{3,19},{19,3},{4,20},{20... | collective-permute-start | bytes 294920 | tf_op jit(solution)/shard_map/ppermute | solution.py:35
  74.3 4.8 %collective-permute-done.6 = f32[1,192,128]{2,1,0:T(8,128)S(1)} collective-permute-done((f32[1,192,128]{2,1,0:T(8,128)S(1)}, f32[1,192,128]{2,1,0:T(8,128)S(1)}, u32[]{:S(2)}, u32[]{:S(2)}) %collective-permute-start.6) | collective-permute-done | bytes 98336 | tf_op jit(solution)/shard_map/ppermute | solution.py:35
  79.2 1.7 fusion.22
  82.3 5.4 %collective-permute-start.7 = (bf16[192,1536]{1,0:T(8,128)(2,1)}, bf16[192,1536]{1,0:T(8,128)(2,1)}, u32[]{:S(2)}, u32[]{:S(2)}) collective-permute-start(bf16[192,1536]{1,0:T(8,128)(2,1)} %get-tuple-element.15), channel_id=1, source_target_pairs={{0,1},{1,2},{2,3},{3,4},{4,5},{5,6},{6,7},{7,8},{8,9},{9,10},{10,1... | collective-permute-start | bytes 1769480 | tf_op jit(solution)/shard_map/ppermute | solution.py:19
  87.7 2.5 %convolution_bitcast_fusion.5 = f32[5,192,128]{2,1,0:T(8,128)} fusion(bf16[5,1536,128]{2,1,0:T(8,128)(2,1)S(1)} %copy-done, bf16[192,1536]{1,0:T(8,128)(2,1)} %get-tuple-element.15), kind=kOutput, calls=%fused_computation.17 | convolution fusion | flops 377487360 | bytes 3047424 | tf_op jit(solution)/shard_map/xp,lpr->lxr/dot_general | solution.py:70
  91.6 8.4 %gather_fusion.1 = f32[1536]{0:T(1024)S(1)} fusion(f32[1536]{0:T(1024)S(1)} %copy-done.2, s32[2048]{0:T(1024)S(1)} %pad_clamp_fusion), kind=kCustom, calls=%fused_computation.3 | custom fusion | bytes 18432 | tf_op jit(solution)/shard_map/jit(_take)/gather | solution.py:111
  100.6 19.1 %collective-permute-done.9 = f32[5,192,128]{2,1,0:T(8,128)} collective-permute-done((f32[5,192,128]{2,1,0:T(8,128)}, f32[5,192,128]{2,1,0:T(8,128)}, u32[]{:S(2)}, u32[]{:S(2)}) %collective-permute-start.9) | collective-permute-done | bytes 491552 | tf_op jit(solution)/shard_map/ppermute | solution.py:35
  121.7 2.7 %pad_maximum_fusion.1 = bf16[192,4608]{1,0:T(8,128)(2,1)} fusion(bf16[192,1536]{1,0:T(8,128)(2,1)} %collective-permute-done.8, bf16[192,1536]{1,0:T(8,128)(2,1)} %get-tuple-element.15, bf16[192,1536]{1,0:T(8,128)(2,1)} %collective-permute-done.7), kind=kLoop, calls=%fused_computation.13 | loop fusion | flops 5308416 | bytes 3538944 | tf_op jit(solution)/shard_map/concatenate | solution.py:17
  124.4 4.0 %copy.42 = bf16[192,4608]{0,1:T(8,128)(2,1)} copy(bf16[192,4608]{1,0:T(8,128)(2,1)} %pad_maximum_fusion.1) | data formatting | bytes 3538944 | tf_op jit(solution)/shard_map/concatenate | solution.py:17
  128.4 4.0 %copy.43 = bf16[192,9,512]{2,0,1:T(8,128)(2,1)} copy(bf16[192,9,512]{0,2,1:T(8,128)(2,1)} %bitcast.61) | data formatting | bytes 3538944 | tf_op jit(solution)/shard_map/reshape | solution.py:43
  132.5 3.8 %gather_fusion.4 = bf16[12,192,512]{2,1,0:T(8,128)(2,1)} fusion(bf16[192,9,512]{2,0,1:T(8,128)(2,1)} %copy.43, s32[1024]{0:T(1024)} %copy-done.11), kind=kCustom, calls=%fused_computation.1.clone | custom fusion | bytes 4718640 | tf_op jit(solution)/shard_map/jit(_take)/gather | solution.py:46
  138.8 2.0 broadcast_select_fusion
  140.9 1.5 collective-permute-start.12
  142.4 5.0 %convolution_bitcast_fusion.2 = f32[3,24,8,512]{3,2,1,0:T(8,128)S(1)} fusion(bf16[192,3,4,512]{3,0,2,1:T(8,128)(2,1)S(1)} %bitcast.58, bf16[3,4,512,512]{3,2,1,0:T(8,128)(2,1)} %param.14), kind=kOutput, calls=%fused_computation.14 | convolution fusion | flops 1207959552 | bytes 9830400 | tf_op jit(solution)/shard_map/bkij,xbkj->xbi/dot_general | solution.py:48
  148.0 3.4 %collective-permute-start.13 = (f32[1,192,128]{2,1,0:T(8,128)S(1)}, f32[1,192,128]{2,1,0:T(8,128)S(1)}, u32[]{:S(2)}, u32[]{:S(2)}) collective-permute-start(f32[1,192,128]{2,1,0:T(8,128)S(1)} %slice.108), channel_id=1, source_target_pairs={{0,16},{16,0},{1,17},{17,1},{2,18},{18,2},{3,19},{19,3},{4,20},{20... | collective-permute-start | bytes 294920 | tf_op jit(solution)/shard_map/ppermute | solution.py:35
  151.5 5.0 %collective-permute-done.13 = f32[1,192,128]{2,1,0:T(8,128)S(1)} collective-permute-done((f32[1,192,128]{2,1,0:T(8,128)S(1)}, f32[1,192,128]{2,1,0:T(8,128)S(1)}, u32[]{:S(2)}, u32[]{:S(2)}) %collective-permute-start.13) | collective-permute-done | bytes 98336 | tf_op jit(solution)/shard_map/ppermute | solution.py:35
  157.7 39.3 %all-reduce = (f32[64]{0:T(128)S(1)}, f32[64]{0:T(128)S(1)}) all-reduce(f32[64]{0:T(128)S(1)} %reduce_sum.37, f32[64]{0:T(128)S(1)} %reduce_sum.25), channel_id=1, replica_groups=mesh['wide'=8,'narrow'=4] {'wide','narrow'}, use_global_device_ids=true, to_apply=%region_5.7 | all-reduce | flops 128 | bytes 1024 | tf_op jit(solution)/shard_map/psum | solution.py:121
  197.0 1.5 multiply_subtract_fusion
  (103 shorter events, 20.4 us)
Async XLA Ops:
  0.6 9.2 %copy-start = (bf16[5,1536,128]{2,1,0:T(8,128)(2,1)S(1)}, bf16[5,1536,128]{2,1,0:T(8,128)(2,1)}, u32[]{:S(2)}) copy-start(bf16[5,1536,128]{2,1,0:T(8,128)(2,1)} %param.16) | copy-start | bytes 5898244
  2.1 11.2 %copy-start.9 = (f32[3,1536]{1,0:T(4,128)S(1)}, f32[3,1536]{1,0:T(4,128)}, u32[]{:S(2)}) copy-start(f32[3,1536]{1,0:T(4,128)} %param.17) | copy-start | bytes 55300
  2.1 43.5 %collective-permute-start.1 = (bf16[192,1536]{1,0:T(8,128)(2,1)S(1)}, bf16[192,1536]{1,0:T(8,128)(2,1)}, u32[]{:S(2)}, u32[]{:S(2)}) collective-permute-start(bf16[192,1536]{1,0:T(8,128)(2,1)S(1)} %bitcast.62), channel_id=1, source_target_pairs={{1,0},{2,1},{3,2},{4,3},{5,4},{6,5},{7,6},{8,7},{9,8},{10,9},{11,1... | collective-permute-start | bytes 1769480 | tf_op jit(solution)/shard_map/ppermute | solution.py:21
  3.4 42.2 %collective-permute-start = (bf16[192,1536]{1,0:T(8,128)(2,1)S(1)}, bf16[192,1536]{1,0:T(8,128)(2,1)}, u32[]{:S(2)}, u32[]{:S(2)}) collective-permute-start(bf16[192,1536]{1,0:T(8,128)(2,1)S(1)} %bitcast.63), channel_id=1, source_target_pairs={{0,1},{1,2},{2,3},{3,4},{4,5},{5,6},{6,7},{7,8},{8,9},{9,10},{10,1... | collective-permute-start | bytes 1769480 | tf_op jit(solution)/shard_map/ppermute | solution.py:19
  9.8 3.8 %copy-start.8 = (s32[1536]{0:T(1024)S(1)}, s32[1536]{0:T(1024)}, u32[]{:S(2)}) copy-start(s32[1536]{0:T(1024)} %param.20) | copy-start | bytes 18436
  9.8 7.6 %copy-start.1 = (s32[1536]{0:T(1024)S(1)}, s32[1536]{0:T(1024)}, u32[]{:S(2)}) copy-start(s32[1536]{0:T(1024)} %param.19) | copy-start | bytes 18436
  11.2 32.4 %collective-permute-start.2 = (f32[5,192,128]{2,1,0:T(8,128)}, f32[5,192,128]{2,1,0:T(8,128)}, u32[]{:S(2)}, u32[]{:S(2)}) collective-permute-start(f32[5,192,128]{2,1,0:T(8,128)} %convolution_bitcast_fusion.4), channel_id=1, source_target_pairs={{0,1},{1,0},{2,3},{3,2},{4,5},{5,4},{6,7},{7,6},{8,9},{9,8},{10,11... | collective-permute-start | bytes 1474568 | tf_op jit(solution)/shard_map/ppermute | solution.py:35
  17.4 8.4 %copy-start.10 = (s32[3,4]{1,0:T(4,128)S(1)}, s32[3,4]{1,0:T(4,128)}, u32[]{:S(2)}) copy-start(s32[3,4]{1,0:T(4,128)} %param.15) | copy-start | bytes 148
  25.7 1.9 copy-start.14
  29.0 27.3 %copy-start.11 = (s32[1024]{0:T(1024)}, s32[1024]{0:T(1024)S(1)}, u32[]{:S(2)}) copy-start(s32[1024]{0:T(1024)S(1)} %pad_clamp_fusion.1) | copy-start | bytes 12292
  29.0 32.3 %copy-start.12 = (pred[12]{0:T(512)(128)(4,1)}, pred[12]{0:T(512)(128)(4,1)S(1)}, u32[]{:S(2)}) copy-start(pred[12]{0:T(512)(128)(4,1)S(1)} %compare_and_fusion.1) | copy-start | bytes 40
  44.8 15.1 %copy-start.6 = (f32[5,192,128]{2,1,0:T(8,128)}, f32[5,192,128]{2,1,0:T(8,128)S(1)}, u32[]{:S(2)}) copy-start(f32[5,192,128]{2,1,0:T(8,128)S(1)} %add.118) | copy-start | bytes 1474564
  44.9 15.1 %collective-permute-start.3 = (f32[4,192,128]{2,1,0:T(8,128)S(1)}, f32[4,192,128]{2,1,0:T(8,128)}, u32[]{:S(2)}, u32[]{:S(2)}) collective-permute-start(f32[4,192,128]{2,1,0:T(8,128)S(1)} %slice.100), channel_id=1, source_target_pairs={{0,2},{2,0},{1,3},{3,1},{4,6},{6,4},{5,7},{7,5},{8,10},{10,8},{9,1... | collective-permute-start | bytes 1179656 | tf_op jit(solution)/shard_map/ppermute | solution.py:35
  61.1 2.3 %collective-permute-start.4 = (f32[3,192,128]{2,1,0:T(8,128)S(1)}, f32[3,192,128]{2,1,0:T(8,128)S(1)}, u32[]{:S(2)}, u32[]{:S(2)}) collective-permute-start(f32[3,192,128]{2,1,0:T(8,128)S(1)} %slice.101), channel_id=1, source_target_pairs={{0,4},{4,0},{1,5},{5,1},{2,6},{6,2},{3,7},{7,3},{8,12},{12,8},{9,1... | collective-permute-start | bytes 884744 | tf_op jit(solution)/shard_map/ppermute | solution.py:35
  63.4 8.0 %collective-permute-start.5 = (f32[2,192,128]{2,1,0:T(8,128)S(1)}, f32[2,192,128]{2,1,0:T(8,128)S(1)}, u32[]{:S(2)}, u32[]{:S(2)}) collective-permute-start(f32[2,192,128]{2,1,0:T(8,128)S(1)} %slice.102), channel_id=1, source_target_pairs={{0,8},{8,0},{1,9},{9,1},{2,10},{10,2},{3,11},{11,3},{4,12},{12,4},... | collective-permute-start | bytes 589832 | tf_op jit(solution)/shard_map/ppermute | solution.py:35
  70.8 3.5 %slice-start.1 = ((f32[5,192,128]{2,1,0:T(8,128)}), f32[1,192,128]{2,1,0:T(8,128)S(1)}, s32[]{:S(2)}) async-start(f32[5,192,128]{2,1,0:T(8,128)} %copy-done.6), calls=%async_computation.1 | async-start | bytes 196608 | tf_op jit(solution)/shard_map/slice | solution.py:57
  70.9 8.3 %copy-start.4 = (f32[192,1536]{1,0:T(8,128)S(1)}, f32[192,1536]{1,0:T(8,128)}, u32[]{:S(2)}) copy-start(f32[192,1536]{1,0:T(8,128)} %bitcast_subtract_fusion) | copy-start | bytes 3538948
  70.9 8.3 %copy-start.15 = (f32[5]{0:T(128)S(1)}, f32[5]{0:T(128)}, u32[]{:S(2)}) copy-start(f32[5]{0:T(128)} %constant.79.clone) | copy-start | bytes 64
  71.5 7.7 %collective-permute-start.6 = (f32[1,192,128]{2,1,0:T(8,128)S(1)}, f32[1,192,128]{2,1,0:T(8,128)S(1)}, u32[]{:S(2)}, u32[]{:S(2)}) collective-permute-start(f32[1,192,128]{2,1,0:T(8,128)S(1)} %slice.103), channel_id=1, source_target_pairs={{0,16},{16,0},{1,17},{17,1},{2,18},{18,2},{3,19},{19,3},{4,20},{20... | collective-permute-start | bytes 294920 | tf_op jit(solution)/shard_map/ppermute | solution.py:35
  80.8 116.2 %copy-start.3 = (f32[192,1536]{1,0:T(8,128)}, f32[192,1536]{1,0:T(8,128)S(1)}, u32[]{:S(2)}) copy-start(f32[192,1536]{1,0:T(8,128)S(1)} %get-tuple-element.16) | copy-start | bytes 3538948
  80.9 10.7 %copy-start.2 = (f32[1536]{0:T(1024)S(1)}, f32[1536]{0:T(1024)}, u32[]{:S(2)}) copy-start(f32[1536]{0:T(1024)} %param.18) | copy-start | bytes 18436
  80.9 40.8 %collective-permute-start.8 = (bf16[192,1536]{1,0:T(8,128)(2,1)}, bf16[192,1536]{1,0:T(8,128)(2,1)}, u32[]{:S(2)}, u32[]{:S(2)}) collective-permute-start(bf16[192,1536]{1,0:T(8,128)(2,1)} %get-tuple-element.15), channel_id=1, source_target_pairs={{1,0},{2,1},{3,2},{4,3},{5,4},{6,5},{7,6},{8,7},{9,8},{10,9},{11,1... | collective-permute-start | bytes 1769480 | tf_op jit(solution)/shard_map/ppermute | solution.py:21
  82.3 39.4 %collective-permute-start.7 = (bf16[192,1536]{1,0:T(8,128)(2,1)}, bf16[192,1536]{1,0:T(8,128)(2,1)}, u32[]{:S(2)}, u32[]{:S(2)}) collective-permute-start(bf16[192,1536]{1,0:T(8,128)(2,1)} %get-tuple-element.15), channel_id=1, source_target_pairs={{0,1},{1,2},{2,3},{3,4},{4,5},{5,6},{6,7},{7,8},{8,9},{9,10},{10,1... | collective-permute-start | bytes 1769480 | tf_op jit(solution)/shard_map/ppermute | solution.py:19
  90.2 29.5 %collective-permute-start.9 = (f32[5,192,128]{2,1,0:T(8,128)}, f32[5,192,128]{2,1,0:T(8,128)}, u32[]{:S(2)}, u32[]{:S(2)}) collective-permute-start(f32[5,192,128]{2,1,0:T(8,128)} %convolution_bitcast_fusion.5), channel_id=1, source_target_pairs={{0,1},{1,0},{2,3},{3,2},{4,5},{5,4},{6,7},{7,6},{8,9},{9,8},{10,11... | collective-permute-start | bytes 1474568 | tf_op jit(solution)/shard_map/ppermute | solution.py:35
  121.7 14.6 %collective-permute-start.10 = (f32[4,192,128]{2,1,0:T(8,128)S(1)}, f32[4,192,128]{2,1,0:T(8,128)}, u32[]{:S(2)}, u32[]{:S(2)}) collective-permute-start(f32[4,192,128]{2,1,0:T(8,128)S(1)} %slice.105), channel_id=1, source_target_pairs={{0,2},{2,0},{1,3},{3,1},{4,6},{6,4},{5,7},{7,5},{8,10},{10,8},{9,1... | collective-permute-start | bytes 1179656 | tf_op jit(solution)/shard_map/ppermute | solution.py:35
  136.3 2.6 %copy-start.13 = (pred[12]{0:T(512)(128)(4,1)S(1)}, pred[12]{0:T(512)(128)(4,1)}, u32[]{:S(2)}) copy-start(pred[12]{0:T(512)(128)(4,1)} %copy-done.12) | copy-start | bytes 40
  137.5 3.3 %collective-permute-start.11 = (f32[3,192,128]{2,1,0:T(8,128)S(1)}, f32[3,192,128]{2,1,0:T(8,128)S(1)}, u32[]{:S(2)}, u32[]{:S(2)}) collective-permute-start(f32[3,192,128]{2,1,0:T(8,128)S(1)} %slice.106), channel_id=1, source_target_pairs={{0,4},{4,0},{1,5},{5,1},{2,6},{6,2},{3,7},{7,3},{8,12},{12,8},{9,1... | collective-permute-start | bytes 884744 | tf_op jit(solution)/shard_map/ppermute | solution.py:35
  140.9 7.1 %collective-permute-start.12 = (f32[2,192,128]{2,1,0:T(8,128)S(1)}, f32[2,192,128]{2,1,0:T(8,128)S(1)}, u32[]{:S(2)}, u32[]{:S(2)}) collective-permute-start(f32[2,192,128]{2,1,0:T(8,128)S(1)} %slice.107), channel_id=1, source_target_pairs={{0,8},{8,0},{1,9},{9,1},{2,10},{10,2},{3,11},{11,3},{4,12},{12,4},... | collective-permute-start | bytes 589832 | tf_op jit(solution)/shard_map/ppermute | solution.py:35
  147.4 4.1 %slice-start = ((f32[5,192,128]{2,1,0:T(8,128)}), f32[1,192,128]{2,1,0:T(8,128)S(1)}, s32[]{:S(2)}) async-start(f32[5,192,128]{2,1,0:T(8,128)} %copy-done.5), calls=%async_computation | async-start | bytes 196608 | tf_op jit(solution)/shard_map/slice | solution.py:57
  147.4 9.1 %copy-start.16 = (f32[5]{0:T(128)S(1)}, f32[5]{0:T(128)}, u32[]{:S(2)}) copy-start(f32[5]{0:T(128)} %constant.79.clone) | copy-start | bytes 64
  148.0 8.4 %collective-permute-start.13 = (f32[1,192,128]{2,1,0:T(8,128)S(1)}, f32[1,192,128]{2,1,0:T(8,128)S(1)}, u32[]{:S(2)}, u32[]{:S(2)}) collective-permute-start(f32[1,192,128]{2,1,0:T(8,128)S(1)} %slice.108), channel_id=1, source_target_pairs={{0,16},{16,0},{1,17},{17,1},{2,18},{18,2},{3,19},{19,3},{4,20},{20... | collective-permute-start | bytes 294920 | tf_op jit(solution)/shard_map/ppermute | solution.py:35
  197.0 1.5 copy-start.7
  (2 other events, 2.3 us)
where the time goes:
time: 201 us; the launch traced here: 200 us
  local copies, waits for them, and re-layouts  46.2 us (23%)
  waiting for transfers between devices  44.4 us (22%)
  blocking collectives  39.3 us (20%)
  starting transfers between devices  30.7 us (15%)
  other arithmetic  21.9 us (11%)
  matrix products  16.5 us (8%)
    ppermute x10, waiting for transfers between devices, from_partner(): return lax.ppermute(block, axis, route)  44.4 us
    psum x1, blocking collectives, body(): lax.psum((cross_local, square_local), ('wide', 'narrow'))  39.3 us
    ppermute x10, starting transfers between devices, from_partner(): return lax.ppermute(block, axis, route)  16.2 us
    ppermute x2, starting transfers between devices, extended(): lax.ppermute(tail, axis, [(i, (i + 1) % count) for i in range(ends)])  11.7 us
    dot_general x2, matrix products, near_field(): jnp.einsum('bkij,xbkj->xbi', near_kernel, picked, preferred_element_type=...  9.91 us
    gather x1, local copies, waits for them, and re-layouts, body(): live_mask = jnp.take(contact_flags, local_order).astype(jnp.float32)  8.38 us
    gather x1, local copies, waits for them, and re-layouts, body(): mu_sorted = jnp.take(friction, local_order)  8.38 us
    reshape x2, local copies, waits for them, and re-layouts, near_field(): blocks = padded.reshape(row_count, 3 * blk_dev, block_len)  8.08 us
  transfers between devices with their start and end apart: 14, of which 6 were waited for; matrix products, arithmetic and copies ran while one was open for 37% of the time, Pallas kernels for 0%

commit v1 on v0

v1 whole, which is shorter than its diff:
```python
import functools
import math

import jax
import jax.numpy as jnp
from jax import lax
from jax.experimental import pallas as pl
from jax.experimental.pallas import tpu as pltpu
from jax.sharding import PartitionSpec as P

SLIP_EPS = 0.01
MESH = pl.DeviceIdType.MESH
GROUP_BITS = 3


def dot(a, b):
    return lax.dot_general(a, b, (((1,), (0,)), ((), ())), preferred_element_type=jnp.float32)


def dot_t(a, b):
    return lax.dot_general(a, b, (((1,), (1,)), ((), ())), preferred_element_type=jnp.float32)


def flip(me, mask):
    peer = me
    bit = 1
    while bit <= mask:
        if mask & bit:
            peer = peer + bit - 2 * bit * ((me // bit) % 2)
        bit *= 2
    return peer


def event_order(chunks, stages):
    step, lead = 6.0, 13.0
    events = []
    for a in range(2):
        for c in range(chunks):
            start = a * lead + c * step
            for s in range(stages):
                events.append((start + 3.0 + 1.8 * s, "tree", a, c, s))
            events.append((start + 5.9, "forward", a, c, 0))
            events.append((start + lead, "finish", a, c, 0))
    return [event[1:] for event in sorted(events, key=lambda event: event[0])]


def kernel(cfg, *refs):
    comps, loads, panels, blocks, near, size, levels, rank, wide, narrow = cfg
    refs = list(refs)
    take = lambda count: [refs.pop(0) for _ in range(count)]
    nb, trac_h, near_h, far_h, gap, fric, flags, order, approach = take(9)
    new_h, res_h, step_ref = take(3)
    trac, kv, bcat, res, table, gs, coef, acc, sums = take(9)
    halos = [take(comps) for _ in range(2)]
    sends, recvs = take(levels), take(levels)
    devices = wide * narrow
    bits = levels
    groups = [(low, min(GROUP_BITS, bits - low)) for low in range(0, bits, GROUP_BITS)]
    slots = take(len(groups))
    load_sem, out_sem, tree_ss, tree_rs, x_ss, x_rs, y_ss, y_rs, stat_ss, stat_rs = take(10)

    me = lax.axis_index("wide") * narrow + lax.axis_index("narrow")
    odd = me % 2
    pair = flip(me, 1)
    onward = me + 2 - 4 * odd
    source = me - 2 + 4 * odd
    has_onward = (onward >= 0) & (onward < devices)
    has_source = (source >= 0) & (source < devices)

    def coords(peer):
        return (peer // narrow, peer % narrow)

    def remote(src, dst, ss, rs, peer):
        return pltpu.make_async_remote_copy(
            src_ref=src, dst_ref=dst, send_sem=ss, recv_sem=rs, device_id=coords(peer), device_id_type=MESH
        )

    trac_in = [pltpu.make_async_copy(trac_h.at[c], trac.at[c], load_sem.at[c]) for c in range(comps)]
    far_in = [
        pltpu.make_async_copy(far_h.at[m], bcat.at[:, m * rank : (m + 1) * rank], load_sem.at[comps + m])
        for m in range(levels)
    ]
    near_in = pltpu.make_async_copy(near_h, kv, load_sem.at[comps + levels])
    for copy in trac_in + far_in:
        copy.start()
    near_in.start()

    masks = set(1 << s for s in range(bits))
    for low, count in groups:
        masks |= set(m << low for m in range(1, 1 << count))
    barrier = pltpu.get_barrier_semaphore()
    for mask in sorted(masks):
        pl.semaphore_signal(barrier, inc=1, device_id=coords(flip(me, mask)), device_id_type=MESH)

    @pl.when(has_onward)
    def _():
        pl.semaphore_signal(barrier, inc=1, device_id=coords(onward), device_id_type=MESH)

    @pl.when(has_source)
    def _():
        pl.semaphore_signal(barrier, inc=1, device_id=coords(source), device_id_type=MESH)

    for a in range(2):
        for c in range(comps):

            @pl.when(me == 0)
            def _():
                halos[a][c][0:blocks] = jnp.zeros((blocks, loads, size), jnp.bfloat16)

            @pl.when(me == devices - 1)
            def _():
                halos[a][c][2 * blocks : 3 * blocks] = jnp.zeros((blocks, loads, size), jnp.bfloat16)

    for c in range(comps):
        trac_in[c].wait()
        for b in range(blocks):
            halos[0][c][blocks + b] = trac[c, :, b * size : (b + 1) * size].astype(jnp.bfloat16)
    for copy in far_in:
        copy.wait()

    def tree_copy(a, c, s):
        return remote(
            sends[s].at[a, c], recvs[s].at[a, c], tree_ss.at[a, c, s], tree_rs.at[a, c, s], flip(me, 1 << s)
        )

    def x_copy(a, c):
        halo = halos[a][c]
        return remote(
            halo.at[pl.ds(blocks, blocks)],
            halo.at[pl.ds((1 - odd) * 0 + odd * 2 * blocks, blocks)],
            x_ss.at[a, c],
            x_rs.at[a, c],
            pair,
        )

    def y_copy(a, c):
        halo = halos[a][c]
        return remote(
            halo.at[pl.ds((1 - odd) * 2 * blocks, blocks)],
            halo.at[pl.ds(odd * 2 * blocks, blocks)],
            y_ss.at[a, c],
            y_rs.at[a, c],
            onward,
        )

    def project(a, c):
        total = dot(halos[a][c][blocks], bcat[0:size, :])
        for b in range(1, blocks):
            total = total + dot(halos[a][c][blocks + b], bcat[b * size : (b + 1) * size, :])
        acc[c] = total
        sends[0][a, c] = total.astype(jnp.bfloat16)

    def launch(a, c):
        tree_copy(a, c, 0).start()
        x_copy(a, c).start()

    for c in range(comps):
        project(0, c)
        if c == 0:
            pl.semaphore_wait(
                barrier, len(masks) + jnp.where(has_onward, 1, 0) + jnp.where(has_source, 1, 0)
            )
        launch(0, c)

    table[...] = jnp.zeros_like(table)
    table[0:comps] = gap[...]
    table[comps : comps + 1] = fric[...]
    table[comps + 1 : comps + 2] = flags[...].astype(jnp.float32)
    whole = table[...]
    high = whole.astype(jnp.bfloat16).astype(jnp.float32)
    rest = whole - high
    middle = rest.astype(jnp.bfloat16).astype(jnp.float32)
    parts = jnp.concatenate([high, middle, rest - middle, jnp.zeros_like(whole)], axis=0).astype(jnp.bfloat16)

    def gather(b, carry):
        cols = pl.ds(pl.multiple_of(b * size, size), size)
        wanted = order[:, cols] - me * panels
        chosen = lax.broadcasted_iota(jnp.int32, (panels, size), 0) == wanted
        picked = dot(parts, chosen.astype(jnp.float32).astype(jnp.bfloat16))
        rows = whole.shape[0]
        gs[:, cols] = picked[0:rows] + picked[rows : 2 * rows] + picked[2 * rows : 3 * rows]
        return carry

    lax.fori_loop(0, blocks, gather, 0)

    diagonal = lax.broadcasted_iota(jnp.int32, (loads, loads), 0) == lax.broadcasted_iota(
        jnp.int32, (loads, loads), 1
    )

    def as_column(row):
        return jnp.sum(jnp.where(diagonal, row, 0.0), axis=1, keepdims=True)

    def as_row(column):
        return jnp.sum(jnp.where(diagonal, column, 0.0), axis=0, keepdims=True)

    columns = [as_column(approach[c : c + 1, :]) for c in range(comps)]
    near_in.wait()

    def tree(a, c, s):
        tree_copy(a, c, s).wait()
        merged = acc[c, :, s * rank :] + recvs[s][a, c].astype(jnp.float32)
        gain = 0.64 / math.sqrt(rank * panels * 2 ** (s + 1))
        coef[c, :, s * rank : (s + 1) * rank] = (merged[:, 0:rank] * gain).astype(jnp.bfloat16)
        if s + 1 < levels:
            acc[c, :, (s + 1) * rank :] = merged[:, rank:]
            sends[s + 1][a, c] = merged[:, rank:].astype(jnp.bfloat16)
            tree_copy(a, c, s + 1).start()

    def forward(a, c):
        x_copy(a, c).wait()

        @pl.when(has_onward)
        def _():
            y_copy(a, c).start()

    def finish(a, c):
        @pl.when(has_source)
        def _():
            y_copy(a, c).wait_recv()

        halo = halos[a][c]

        def block(b, carry):
            cols = pl.ds(pl.multiple_of(b * size, size), size)
            total = dot_t(coef[c], bcat[cols, :])
            for k in range(near):
                slot = nb[b, k] - nb[b, 0] + b + blocks
                total = total + dot_t(halo[slot], kv[b, k])
            if a == 0:
                value = total - (columns[c] - gs[c : c + 1, cols])
                res[c, :, cols] = value
                halos[1][c][blocks + b] = value.astype(jnp.bfloat16)
                return carry
            cross, square = carry
            cross = cross + jnp.sum(res[c, :, cols] * total, axis=1, keepdims=True)
            return cross, square + jnp.sum(total * total, axis=1, keepdims=True)

        if a == 0:
            lax.fori_loop(0, blocks, block, 0)
            project(1, c)
            launch(1, c)
            pltpu.make_async_copy(res.at[c], res_h.at[c], out_sem.at[0, c]).start()
            return None
        zero = jnp.zeros((loads, 1), jnp.float32)
        return lax.fori_loop(0, blocks, block, (zero, zero))

    cross = square = None
    for kind, a, c, s in event_order(comps, levels):
        if kind == "tree":
            tree(a, c, s)
        elif kind == "forward":
            forward(a, c)
        else:
            part = finish(a, c)
            if a == 1:
                cross = part[0] if cross is None else cross + part[0]
                square = part[1] if square is None else square + part[1]

    sums[...] = jnp.zeros_like(sums)
    sums[0:1, 0:loads] = as_row(cross)
    sums[1:2, 0:loads] = as_row(square)
    for g, (low, count) in enumerate(groups):
        slot = slots[g]
        mine = (me // (1 << low)) % (1 << count)
        slot[mine] = sums[...]
        copies = []
        for m in range(1, 1 << count):
            copies.append(
                remote(slot.at[mine], slot.at[mine], stat_ss.at[g, m], stat_rs.at[g, m], flip(me, m << low))
            )
            copies[-1].start()
        for copy in copies:
            copy.wait()
        total = slot[0]
        for m in range(1, 1 << count):
            total = total + slot[m]
        sums[...] = total

    entries = comps * panels * devices
    step_row = sums[0:1, 0:loads] / entries / (sums[1:2, 0:loads] / entries + 1e-06)
    step_ref[...] = step_row
    step = as_column(step_row)

    def update(b, carry):
        cols = pl.ds(pl.multiple_of(b * size, size), size)
        normal = trac[0, :, cols] - step * res[0, :, cols]
        slide_a = trac[1, :, cols] - step * res[1, :, cols]
        slide_b = trac[2, :, cols] - step * res[2, :, cols]
        mu = gs[comps : comps + 1, cols]
        live = gs[comps + 1 : comps + 2, cols]
        slip = jnp.sqrt(slide_a * slide_a + slide_b * slide_b + SLIP_EPS)
        stick = slip <= mu * normal
        pressed = jnp.where(stick, normal, jnp.maximum((normal + mu * slip) / (1.0 + mu * mu), 0.0))
        factor = jnp.where(stick, jnp.ones_like(slip), mu * pressed / slip)
        trac[0, :, cols] = pressed * live
        trac[1, :, cols] = factor * slide_a * live
        trac[2, :, cols] = factor * slide_b * live
        return carry

    lax.fori_loop(0, blocks, update, 0)
    outs = [pltpu.make_async_copy(trac.at[c], new_h.at[c], out_sem.at[1, c]) for c in range(comps)]
    for copy in outs:
        copy.start()
    for a in range(2):
        for c in range(comps):

            @pl.when(has_onward)
            def _():
                y_copy(a, c).wait_send()

    for c in range(comps):
        pltpu.make_async_copy(res.at[c], res_h.at[c], out_sem.at[0, c]).wait()
        outs[c].wait()


def body(wide, narrow, traction, near_kernel, neighbours, far_basis, surface_gap, friction, flags, order, approach):
    comps, loads, panels = traction.shape
    blocks, near, size = near_kernel.shape[:3]
    levels, _, rank = far_basis.shape
    cfg = (comps, loads, panels, blocks, near, size, levels, rank, wide, narrow)
    low = jnp.bfloat16
    groups = [min(GROUP_BITS, levels - at) for at in range(0, levels, GROUP_BITS)]
    dma = pltpu.SemaphoreType.DMA
    vmem = pl.BlockSpec(memory_space=pltpu.VMEM)
    anywhere = pl.BlockSpec(memory_space=pl.ANY)
    scratch = [
        pltpu.VMEM(traction.shape, jnp.float32),
        pltpu.VMEM(near_kernel.shape, low),
        pltpu.VMEM((panels, levels * rank), low),
        pltpu.VMEM(traction.shape, jnp.float32),
        pltpu.VMEM((8, panels), jnp.float32),
        pltpu.VMEM((8, panels), jnp.float32),
        pltpu.VMEM((comps, loads, levels * rank), low),
        pltpu.VMEM((comps, loads, levels * rank), jnp.float32),
        pltpu.VMEM((8, 128), jnp.float32),
    ]
    scratch += [pltpu.VMEM((3 * blocks, loads, size), low) for _ in range(2 * comps)]
    for _ in range(2):
        scratch += [pltpu.VMEM((2, comps, loads, (levels - s) * rank), low) for s in range(levels)]
    scratch += [pltpu.VMEM((1 << count, 8, 128), jnp.float32) for count in groups]
    scratch += [dma((comps + levels + 1,)), dma((2, comps))]
    scratch += [dma((2, comps, levels))] * 2 + [dma((2, comps))] * 4
    scratch += [dma((len(groups), 1 << GROUP_BITS))] * 2
    new, residual, step = pl.pallas_call(
        functools.partial(kernel, cfg),
        out_shape=(
            jax.ShapeDtypeStruct(traction.shape, jnp.float32),
            jax.ShapeDtypeStruct(traction.shape, jnp.float32),
            jax.ShapeDtypeStruct((1, loads), jnp.float32),
        ),
        in_specs=[pl.BlockSpec(memory_space=pltpu.SMEM)] + [anywhere] * 3 + [vmem] * 5,
        out_specs=(anywhere, anywhere, vmem),
        scratch_shapes=scratch,
        compiler_params=pltpu.CompilerParams(
            collective_id=0, has_side_effects=True, vmem_limit_bytes=50 * 1024 * 1024
        ),
    )(
        neighbours,
        traction,
        near_kernel,
        far_basis,
        surface_gap,
        friction.reshape(1, panels),
        flags.reshape(1, panels),
        order.reshape(1, panels),
        approach,
    )
    return new, residual, step.reshape(loads)


def solution(mesh):
    sizes = mesh.shape
    return jax.shard_map(
        functools.partial(body, sizes["wide"], sizes["narrow"]),
        mesh=mesh,
        in_specs=(
            P(None, None, ("wide", "narrow")),
            P(("wide", "narrow"), None, None, None),
            P(("wide", "narrow"), None),
            P(None, ("wide", "narrow"), None),
            P(None, ("wide", "narrow")),
            P(("wide", "narrow")),
            P(("wide", "narrow")),
            P(("wide", "narrow")),
            P(),
        ),
        out_specs=(P(None, None, ("wide", "narrow")), P(None, None, ("wide", "narrow")), P()),
        check_vma=False,
    )
```

time: 201 us -> 90.3 us (0.45)
  Pallas kernels: 0 us -> 81.3 us
  waiting for transfers between devices: 44.4 us -> 0 us
  blocking collectives: 39.3 us -> 0 us
  local copies, waits for them, and re-layouts: 46.2 us -> 8.01 us
  starting transfers between devices: 30.7 us -> 0 us
  other arithmetic: 21.9 us -> 0 us
  matrix products: 16.5 us -> 0 us
    pallas_call x0 -> x1, Pallas kernels: none -> 81.3 us  [body(): pl.pallas_call(functools.partial(kernel, cfg), out_shape=(jax.ShapeDtypeS...]
    ppermute x14 -> x0, waiting for transfers between devices: 44.4 us -> none  [the longest x10 44.4 us: from_partner(): return lax.ppermute(block, axis, route)]
    psum x1 -> x0, blocking collectives: 39.3 us -> none  [body(): lax.psum((cross_local, square_local), ('wide', 'narrow'))]
    ppermute x14 -> x0, starting transfers between devices: 30.7 us -> none  [the longest x10 16.2 us: from_partner(): return lax.ppermute(block, axis, route)]
    gather x5 -> x0, local copies, waits for them, and re-layouts: 27.9 us -> none  [the longest x1 8.38 us: body(): live_mask = jnp.take(contact_flags, local_order).astype(jnp.float32)]
    dot_general x6 -> x0, matrix products: 16.5 us -> none  [the longest x2 9.91 us: near_field(): jnp.einsum('bkij,xbkj->xbi', near_kernel, picked, preferred_element_type=...]
    concatenate x2 -> x0, local copies, waits for them, and re-layouts: 7.99 us -> none  [extended(): jnp.concatenate([lax.ppermute(tail, axis, [(i, (i + 1) % count) for i in...]
    reshape x5 -> x3, local copies, waits for them, and re-layouts: 8.33 us -> 2.1 us  [the longest x1 0.7 us: body(): friction.reshape(1, panels)]
  transfers between devices with their start and end apart: 14 -> 0, of which waited for: 6 -> 0; matrix products, arithmetic and copies ran while one was open for 37% -> 0% of each run, Pallas kernels for 0% -> 0%
where the time goes in v1:
time: 90.3 us; the launch traced here: 89.9 us
  Pallas kernels  81.3 us (90%)
  local copies, waits for them, and re-layouts  8.01 us (9%)
    pallas_call x1, Pallas kernels, body(): pl.pallas_call(functools.partial(kernel, cfg), out_shape=(jax.ShapeDtypeS...  81.3 us
    unnamed x11, local copies, waits for them, and re-layouts  5.91 us

profile of v1, /device:TPU:0, one launch (start us, length us, event | category | flops | bytes accessed | tf_op | source)
XLA Modules:
  0.0 89.9 jit_solution(16219792318386314310)
XLA Ops:
  0.6 0.7 reshape.18.refs_5_
  1.3 0.7 reshape.19.refs_6_
  2.0 0.7 reshape.20.refs_7_
  2.7 0.0 copy-start
  2.7 1.3 %copy-done = f32[3,64,1536]{2,1,0:T(8,128)S(1)} copy-done((f32[3,64,1536]{2,1,0:T(8,128)S(1)}, f32[3,64,1536]{2,1,0:T(8,128)}, u32[]{:S(2)}) %copy-start) | copy-done | bytes 1179672
  4.0 0.0 copy-start.1
  4.0 0.7 copy-done.1
  4.7 0.0 copy-start.2
  4.7 0.7 copy-done.2
  5.4 0.0 copy-start.3
  5.4 0.7 copy-done.3
  6.1 81.3 %shard_map.112 = (f32[3,64,1536]{2,1,0:T(8,128)S(1)}, f32[3,64,1536]{2,1,0:T(8,128)S(1)}, f32[1,64]{1,0:T(1,128)S(1)}) custom-call(s32[3,4]{1,0:T(4,128)S(1)} %copy-done.2, f32[3,64,1536]{2,1,0:T(8,128)S(1)} %copy-done, bf16[3,4,512,512]{3,2,1,0:T(8,128)(2,1)} %refs_2_.1, bf16[5,1536,128]{2,1,0:T(8,128)(2,1)} %refs_3_.1, f32[3,1536]{1,0:T(4,128)S(1)} %copy-done.1, ...), custom_call_target="tpu_custom_call" | custom-call | tf_op jit(solution)/shard_map/pallas_call | solution.py:344
  87.4 1.0 %copy.15 = f32[3,64,1536]{2,1,0:T(8,128)} copy(f32[3,64,1536]{2,1,0:T(8,128)S(1)} %get-tuple-element.12) | data formatting | bytes 2359296
  88.4 1.0 %copy.16 = f32[3,64,1536]{2,1,0:T(8,128)} copy(f32[3,64,1536]{2,1,0:T(8,128)S(1)} %get-tuple-element.13) | data formatting | bytes 2359296
  89.4 0.5 copy.17
Async XLA Ops:
  2.7 1.3 %copy-start = (f32[3,64,1536]{2,1,0:T(8,128)S(1)}, f32[3,64,1536]{2,1,0:T(8,128)}, u32[]{:S(2)}) copy-start(f32[3,64,1536]{2,1,0:T(8,128)} %refs_1_.1) | copy-start | bytes 3538948
  4.0 0.7 copy-start.1
  4.7 0.7 copy-start.2
  5.4 0.7 copy-start.3

commit v2 on v1

--- a/solution.py
+++ b/solution.py
@@ -10,7 +10,6 @@
 
 SLIP_EPS = 0.01
 MESH = pl.DeviceIdType.MESH
-GROUP_BITS = 3
 
 
 def dot(a, b):
@@ -32,14 +31,15 @@
 
 
 def event_order(chunks, stages):
-    step, lead = 6.0, 13.0
+    step, lead, first, later, ahead = 4.0, 12.0, 2.0, 3.0, 5.0
     events = []
     for a in range(2):
         for c in range(chunks):
             start = a * lead + c * step
             for s in range(stages):
-                events.append((start + 3.0 + 1.8 * s, "tree", a, c, s))
-            events.append((start + 5.9, "forward", a, c, 0))
+                events.append((start + first + later * s, "tree", a, c, s))
+            events.append((start + lead - 0.1, "upper", a, c, 0))
+            events.append((start + ahead, "forward", a, c, 0))
             events.append((start + lead, "finish", a, c, 0))
     return [event[1:] for event in sorted(events, key=lambda event: event[0])]
 
@@ -51,13 +51,15 @@
     nb, trac_h, near_h, far_h, gap, fric, flags, order, approach = take(9)
     new_h, res_h, step_ref = take(3)
     trac, kv, bcat, res, table, gs, coef, acc, sums = take(9)
+    gap_v, fric_v, flags_v, order_v, approach_v = take(5)
     halos = [take(comps) for _ in range(2)]
-    sends, recvs = take(levels), take(levels)
     devices = wide * narrow
-    bits = levels
-    groups = [(low, min(GROUP_BITS, bits - low)) for low in range(0, bits, GROUP_BITS)]
+    lower = narrow.bit_length() - 1
+    sends, recvs = take(lower + 1), take(lower)
+    upper_in = [None] + take(wide - 1)
+    groups = [(0, lower), (lower, levels - lower)]
     slots = take(len(groups))
-    load_sem, out_sem, tree_ss, tree_rs, x_ss, x_rs, y_ss, y_rs, stat_ss, stat_rs = take(10)
+    load_sem, out_sem, tree_ss, tree_rs, up_ss, up_rs, x_ss, x_rs, y_ss, y_rs, stat_ss, stat_rs = take(12)
 
     me = lax.axis_index("wide") * narrow + lax.axis_index("narrow")
     odd = me % 2
@@ -81,11 +83,16 @@
         for m in range(levels)
     ]
     near_in = pltpu.make_async_copy(near_h, kv, load_sem.at[comps + levels])
-    for copy in trac_in + far_in:
+    small_in = [
+        pltpu.make_async_copy(src, dst, load_sem.at[comps + levels + 1 + i])
+        for i, (src, dst) in enumerate(
+            [(gap, gap_v), (fric, fric_v), (flags, flags_v), (order, order_v), (approach, approach_v)]
+        )
+    ]
+    for copy in trac_in + far_in + small_in:
         copy.start()
-    near_in.start()
-
-    masks = set(1 << s for s in range(bits))
+
+    masks = set()
     for low, count in groups:
         masks |= set(m << low for m in range(1, 1 << count))
     barrier = pltpu.get_barrier_semaphore()
@@ -117,10 +124,21 @@
             halos[0][c][blocks + b] = trac[c, :, b * size : (b + 1) * size].astype(jnp.bfloat16)
     for copy in far_in:
         copy.wait()
+    near_in.start()
 
     def tree_copy(a, c, s):
         return remote(
             sends[s].at[a, c], recvs[s].at[a, c], tree_ss.at[a, c, s], tree_rs.at[a, c, s], flip(me, 1 << s)
+        )
+
+    def upper_copy(a, c, m):
+        skip = (m.bit_length() - 1) * rank
+        return remote(
+            sends[lower].at[a, c, :, skip:],
+            upper_in[m].at[a, c],
+            up_ss.at[a, c, m],
+            up_rs.at[a, c, m],
+            flip(me, m << lower),
         )
 
     def x_copy(a, c):
@@ -163,9 +181,11 @@
         launch(0, c)
 
     table[...] = jnp.zeros_like(table)
-    table[0:comps] = gap[...]
-    table[comps : comps + 1] = fric[...]
-    table[comps + 1 : comps + 2] = flags[...].astype(jnp.float32)
+    for copy in small_in:
+        copy.wait()
+    table[0:comps] = gap_v[...]
+    table[comps : comps + 1] = fric_v[...].reshape(1, panels)
+    table[comps + 1 : comps + 2] = flags_v[...].reshape(1, panels).astype(jnp.float32)
     whole = table[...]
     high = whole.astype(jnp.bfloat16).astype(jnp.float32)
     rest = whole - high
@@ -174,7 +194,7 @@
 
     def gather(b, carry):
         cols = pl.ds(pl.multiple_of(b * size, size), size)
-        wanted = order[:, cols] - me * panels
+        wanted = order_v[cols].reshape(1, size) - me * panels
         chosen = lax.broadcasted_iota(jnp.int32, (panels, size), 0) == wanted
         picked = dot(parts, chosen.astype(jnp.float32).astype(jnp.bfloat16))
         rows = whole.shape[0]
@@ -193,7 +213,7 @@
     def as_row(column):
         return jnp.sum(jnp.where(diagonal, column, 0.0), axis=0, keepdims=True)
 
-    columns = [as_column(approach[c : c + 1, :]) for c in range(comps)]
+    columns = [as_column(approach_v[c : c + 1, :]) for c in range(comps)]
     near_in.wait()
 
     def tree(a, c, s):
@@ -201,10 +221,27 @@
         merged = acc[c, :, s * rank :] + recvs[s][a, c].astype(jnp.float32)
         gain = 0.64 / math.sqrt(rank * panels * 2 ** (s + 1))
         coef[c, :, s * rank : (s + 1) * rank] = (merged[:, 0:rank] * gain).astype(jnp.bfloat16)
-        if s + 1 < levels:
-            acc[c, :, (s + 1) * rank :] = merged[:, rank:]
-            sends[s + 1][a, c] = merged[:, rank:].astype(jnp.bfloat16)
+        acc[c, :, (s + 1) * rank :] = merged[:, rank:]
+        sends[s + 1][a, c] = merged[:, rank:].astype(jnp.bfloat16)
+        if s + 1 < lower:
             tree_copy(a, c, s + 1).start()
+        else:
+            for m in reversed(range(1, wide)):
+                upper_copy(a, c, m).start()
+
+    def upper(a, c):
+        total = acc[c, :, lower * rank :]
+        for u in range(levels - lower):
+            extra = None
+            for m in range(1 << u, 2 << u):
+                upper_copy(a, c, m).wait()
+                piece = upper_in[m][a, c].astype(jnp.float32)
+                extra = piece if extra is None else extra + piece
+            total = total + extra
+            gain = 0.64 / math.sqrt(rank * panels * 2 ** (lower + u + 1))
+            at = (lower + u) * rank
+            coef[c, :, at : at + rank] = (total[:, 0:rank] * gain).astype(jnp.bfloat16)
+            total = total[:, rank:]
 
     def forward(a, c):
         x_copy(a, c).wait()
@@ -245,9 +282,11 @@
         return lax.fori_loop(0, blocks, block, (zero, zero))
 
     cross = square = None
-    for kind, a, c, s in event_order(comps, levels):
+    for kind, a, c, s in event_order(comps, lower):
         if kind == "tree":
             tree(a, c, s)
+        elif kind == "upper":
+            upper(a, c)
         elif kind == "forward":
             forward(a, c)
         else:
@@ -319,7 +358,8 @@
     levels, _, rank = far_basis.shape
     cfg = (comps, loads, panels, blocks, near, size, levels, rank, wide, narrow)
     low = jnp.bfloat16
-    groups = [min(GROUP_BITS, levels - at) for at in range(0, levels, GROUP_BITS)]
+    lower = narrow.bit_length() - 1
+    ranks = lambda s: pltpu.VMEM((2, comps, loads, (levels - s) * rank), low)
     dma = pltpu.SemaphoreType.DMA
     vmem = pl.BlockSpec(memory_space=pltpu.VMEM)
     anywhere = pl.BlockSpec(memory_space=pl.ANY)
@@ -333,14 +373,19 @@
         pltpu.VMEM((comps, loads, levels * rank), low),
         pltpu.VMEM((comps, loads, levels * rank), jnp.float32),
         pltpu.VMEM((8, 128), jnp.float32),
+        pltpu.VMEM(surface_gap.shape, jnp.float32),
+        pltpu.VMEM((panels,), jnp.float32),
+        pltpu.VMEM((panels,), jnp.int32),
+        pltpu.VMEM((panels,), jnp.int32),
+        pltpu.VMEM(approach.shape, jnp.float32),
     ]
     scratch += [pltpu.VMEM((3 * blocks, loads, size), low) for _ in range(2 * comps)]
-    for _ in range(2):
-        scratch += [pltpu.VMEM((2, comps, loads, (levels - s) * rank), low) for s in range(levels)]
-    scratch += [pltpu.VMEM((1 << count, 8, 128), jnp.float32) for count in groups]
-    scratch += [dma((comps + levels + 1,)), dma((2, comps))]
-    scratch += [dma((2, comps, levels))] * 2 + [dma((2, comps))] * 4
-    scratch += [dma((len(groups), 1 << GROUP_BITS))] * 2
+    scratch += [ranks(s) for s in range(lower + 1)] + [ranks(s) for s in range(lower)]
+    scratch += [ranks(lower + m.bit_length() - 1) for m in range(1, wide)]
+    scratch += [pltpu.VMEM((count, 8, 128), jnp.float32) for count in (narrow, wide)]
+    scratch += [dma((comps + levels + 6,)), dma((2, comps))]
+    scratch += [dma((2, comps, lower))] * 2 + [dma((2, comps, wide))] * 2 + [dma((2, comps))] * 4
+    scratch += [dma((2, max(narrow, wide)))] * 2
     new, residual, step = pl.pallas_call(
         functools.partial(kernel, cfg),
         out_shape=(
@@ -348,7 +393,7 @@
             jax.ShapeDtypeStruct(traction.shape, jnp.float32),
             jax.ShapeDtypeStruct((1, loads), jnp.float32),
         ),
-        in_specs=[pl.BlockSpec(memory_space=pltpu.SMEM)] + [anywhere] * 3 + [vmem] * 5,
+        in_specs=[pl.BlockSpec(memory_space=pltpu.SMEM)] + [anywhere] * 8,
         out_specs=(anywhere, anywhere, vmem),
         scratch_shapes=scratch,
         compiler_params=pltpu.CompilerParams(
@@ -360,9 +405,9 @@
         near_kernel,
         far_basis,
         surface_gap,
-        friction.reshape(1, panels),
-        flags.reshape(1, panels),
-        order.reshape(1, panels),
+        friction,
+        flags,
+        order,
         approach,
     )
     return new, residual, step.reshape(loads)

time: 90.3 us -> 78.6 us (0.87)
  Pallas kernels: 81.3 us -> 69.6 us
    pallas_call x1, Pallas kernels: 81.3 us -> 69.6 us  [body(): pl.pallas_call(functools.partial(kernel, cfg), out_shape=(jax.ShapeDtypeS...]
    reshape x3 -> x0, local copies, waits for them, and re-layouts: 2.1 us -> none  [the longest x1 0.7 us: body(): friction.reshape(1, panels)]
    unnamed x11 -> x17, local copies, waits for them, and re-layouts: 5.91 us -> 7.99 us
where the time goes in v2:
time: 78.6 us; the launch traced here: 78.2 us
  Pallas kernels  69.6 us (89%)
  local copies, waits for them, and re-layouts  7.99 us (10%)
    pallas_call x1, Pallas kernels, body(): pl.pallas_call(functools.partial(kernel, cfg), out_shape=(jax.ShapeDtypeS...  69.6 us
    unnamed x17, local copies, waits for them, and re-layouts  7.99 us

profile of v2, /device:TPU:0, one launch (start us, length us, event | category | flops | bytes accessed | tf_op | source)
XLA Modules:
  0.0 78.2 jit_solution(11864477189579437322)
XLA Ops:
  0.6 0.0 copy-start
  0.6 1.3 %copy-done = f32[3,64,1536]{2,1,0:T(8,128)S(1)} copy-done((f32[3,64,1536]{2,1,0:T(8,128)S(1)}, f32[3,64,1536]{2,1,0:T(8,128)}, u32[]{:S(2)}) %copy-start) | copy-done | bytes 1179672
  1.9 0.0 copy-start.1
  1.9 0.7 copy-done.1
  2.6 0.0 copy-start.2
  2.6 0.7 copy-done.2
  3.3 0.0 copy-start.3
  3.3 0.7 copy-done.3
  4.0 0.0 copy-start.4
  4.0 0.7 copy-done.4
  4.7 0.0 copy-start.5
  4.7 0.7 copy-done.5
  5.4 0.0 copy-start.6
  5.4 0.7 copy-done.6
  6.1 69.6 %shard_map.112 = (f32[3,64,1536]{2,1,0:T(8,128)S(1)}, f32[3,64,1536]{2,1,0:T(8,128)S(1)}, f32[1,64]{1,0:T(1,128)S(1)}) custom-call(s32[3,4]{1,0:T(4,128)S(1)} %copy-done.5, f32[3,64,1536]{2,1,0:T(8,128)S(1)} %copy-done, bf16[3,4,512,512]{3,2,1,0:T(8,128)(2,1)} %refs_2_.1, bf16[5,1536,128]{2,1,0:T(8,128)(2,1)} %refs_3_.1, f32[3,1536]{1,0:T(4,128)S(1)} %copy-done.1, ...), custom_call_target="tpu_custom_call" | custom-call | tf_op jit(solution)/shard_map/pallas_call | solution.py:389
  75.7 1.0 %copy.15 = f32[3,64,1536]{2,1,0:T(8,128)} copy(f32[3,64,1536]{2,1,0:T(8,128)S(1)} %get-tuple-element.12) | data formatting | bytes 2359296
  76.7 1.0 %copy.16 = f32[3,64,1536]{2,1,0:T(8,128)} copy(f32[3,64,1536]{2,1,0:T(8,128)S(1)} %get-tuple-element.13) | data formatting | bytes 2359296
  77.7 0.5 copy.17
Async XLA Ops:
  0.6 1.3 %copy-start = (f32[3,64,1536]{2,1,0:T(8,128)S(1)}, f32[3,64,1536]{2,1,0:T(8,128)}, u32[]{:S(2)}) copy-start(f32[3,64,1536]{2,1,0:T(8,128)} %refs_1_.1) | copy-start | bytes 3538948
  1.9 0.7 copy-start.1
  2.6 0.7 copy-start.2
  3.3 0.7 copy-start.3
  4.0 0.7 copy-start.4
  4.7 0.7 copy-start.5
  5.4 0.7 copy-start.6

commit v3 on v2

--- a/solution.py
+++ b/solution.py
@@ -35,7 +35,7 @@
     events = []
     for a in range(2):
         for c in range(chunks):
-            start = a * lead + c * step
+            start = a * (lead + 3.2) + c * step
             for s in range(stages):
                 events.append((start + first + later * s, "tree", a, c, s))
             events.append((start + lead - 0.1, "upper", a, c, 0))

time: 78.6 us -> 79.7 us (1.014)
  Pallas kernels: 69.6 us -> 70.7 us
    pallas_call x1, Pallas kernels: 69.6 us -> 70.7 us  [body(): pl.pallas_call(functools.partial(kernel, cfg), out_shape=(jax.ShapeDtypeS...]
where the time goes in v3:
time: 79.7 us; the launch traced here: 79.3 us
  Pallas kernels  70.7 us (89%)
  local copies, waits for them, and re-layouts  7.99 us (10%)
    pallas_call x1, Pallas kernels, body(): pl.pallas_call(functools.partial(kernel, cfg), out_shape=(jax.ShapeDtypeS...  70.7 us
    unnamed x17, local copies, waits for them, and re-layouts  7.99 us

profile of v3, /device:TPU:0, one launch (start us, length us, event | category | flops | bytes accessed | tf_op | source)
XLA Modules:
  0.0 79.3 jit_solution(16007365623060351465)
XLA Ops:
  0.6 0.0 copy-start
  0.6 1.3 %copy-done = f32[3,64,1536]{2,1,0:T(8,128)S(1)} copy-done((f32[3,64,1536]{2,1,0:T(8,128)S(1)}, f32[3,64,1536]{2,1,0:T(8,128)}, u32[]{:S(2)}) %copy-start) | copy-done | bytes 1179672
  1.9 0.0 copy-start.1
  1.9 0.7 copy-done.1
  2.6 0.0 copy-start.2
  2.6 0.7 copy-done.2
  3.3 0.0 copy-start.3
  3.3 0.7 copy-done.3
  4.0 0.0 copy-start.4
  4.0 0.7 copy-done.4
  4.7 0.0 copy-start.5
  4.7 0.7 copy-done.5
  5.4 0.0 copy-start.6
  5.4 0.7 copy-done.6
  6.1 70.7 %shard_map.112 = (f32[3,64,1536]{2,1,0:T(8,128)S(1)}, f32[3,64,1536]{2,1,0:T(8,128)S(1)}, f32[1,64]{1,0:T(1,128)S(1)}) custom-call(s32[3,4]{1,0:T(4,128)S(1)} %copy-done.5, f32[3,64,1536]{2,1,0:T(8,128)S(1)} %copy-done, bf16[3,4,512,512]{3,2,1,0:T(8,128)(2,1)} %refs_2_.1, bf16[5,1536,128]{2,1,0:T(8,128)(2,1)} %refs_3_.1, f32[3,1536]{1,0:T(4,128)S(1)} %copy-done.1, ...), custom_call_target="tpu_custom_call" | custom-call | tf_op jit(solution)/shard_map/pallas_call | solution.py:389
  76.8 1.0 %copy.15 = f32[3,64,1536]{2,1,0:T(8,128)} copy(f32[3,64,1536]{2,1,0:T(8,128)S(1)} %get-tuple-element.12) | data formatting | bytes 2359296
  77.8 1.0 %copy.16 = f32[3,64,1536]{2,1,0:T(8,128)} copy(f32[3,64,1536]{2,1,0:T(8,128)S(1)} %get-tuple-element.13) | data formatting | bytes 2359296
  78.8 0.5 copy.17
Async XLA Ops:
  0.6 1.3 %copy-start = (f32[3,64,1536]{2,1,0:T(8,128)S(1)}, f32[3,64,1536]{2,1,0:T(8,128)}, u32[]{:S(2)}) copy-start(f32[3,64,1536]{2,1,0:T(8,128)} %refs_1_.1) | copy-start | bytes 3538948
  1.9 0.7 copy-start.1
  2.6 0.7 copy-start.2
  3.3 0.7 copy-start.3
  4.0 0.7 copy-start.4
  4.7 0.7 copy-start.5
  5.4 0.7 copy-start.6
